TPU v7x, 32 devices: a whole 2x2x4 slice. The times are simulated.
32 devices in a mesh: patch: 2 (over y), exp: 4 (over z), tile: 2 (over x), band: 2 (over core).
Axes of the slice: x: 2, y: 2, z: 4, core: 2. Of those that a mesh axis runs over, the one named last changes fastest.
Arguments:
- images: bfloat16 [4, 2, 64, 128, 128], P(('patch', 'band'), 'tile', 'exp'), parts along dimension 0, may hold values from -6 to 6
- mask_bits: int32 [4, 2, 64, 128, 128], P(('patch', 'band'), 'tile', 'exp'), parts along dimension 0, may hold values from 0 to 7
- inv_var: float32 [4, 2, 64], P(('patch', 'band'), 'tile', 'exp'), parts along dimension 0, may hold values from 0.5 to 4
- routes: int32 [4, 2, 64, 1], P(('patch', 'band'), 'tile', 'exp'), parts along dimension 0, may hold values from 0 to 3; in each aligned block of 16 rows (0 to 15, 16 to 31, ..., all dimensions but the last counted through in order) at most 8 rows name the same one
- block_slot: int32 [4, 2, 64], P(('patch', 'band'), 'tile', 'exp'), parts along dimension 0, may hold values from 0 to 7
- kernel_index: int32 [4, 2, 64], P(('patch', 'band'), 'tile', 'exp'), parts along dimension 0, may hold values from 0 to 63
- coefficients: float32 [64, 3], replicated, may hold values from -4 to 4
Outputs:
- coadd: float32 [4, 512, 2048], P(('patch', 'band'), 'tile', 'exp'), parts along dimension 0
- detection: float32 [1024, 2048], P(('patch', 'tile'), 'exp'), parts along dimension 0
There are 2 independent parts, one for each index of `patch`. A program takes and returns all parts, laid end to end along the dimension named above; an argument that names none is the same for every part. Nothing has to cross between parts.
Inputs may be any that keep to these rules, and one draw needn't show every extreme that they name: Among the 16 sub-blocks of one device for one band and strip (an aligned block of routes), no tile column is named more than 8 times, and some tile column is named exactly 8 times.
All inputs are finite; a program needn't handle non-finite values.
Results may differ from a plain program's by a relative error of at most 0.0039.
Values may be sent and summed in bfloat16 or wider, within the bound.
A program may use at most 128 MiB of HBM per device.

v0:
```python
import jax
import jax.numpy as jnp
from jax import lax
from jax.sharding import PartitionSpec as P

BLOCK = 128
TAPS = 41
BLOCK_ROWS = 2
BLOCK_COLS = 4


kernel_sigmas = (1.0, 2.5, 6.0)


def extended(block, sides, width):
    for axis, dim in sides:
        count = lax.axis_size(axis)
        forward = [(i, i + 1) for i in range(count - 1)]
        backward = [(target, source) for source, target in forward]
        low = lax.ppermute(
            lax.slice_in_dim(block, block.shape[dim] - width, None, axis=dim), axis, forward
        )
        high = lax.ppermute(lax.slice_in_dim(block, 0, width, axis=dim), axis, backward)
        block = jnp.concatenate([low, block, high], axis=dim)
    return block


def usable_share(bits):
    flagged = jnp.bitwise_and(bits, 6) == 6
    suspect = jnp.bitwise_and(bits, 1).astype(jnp.float32)
    return jnp.where(flagged, 0.0, 1.0 - 0.5 * suspect)


def band_matrix(length, half_span):
    rows_here = jnp.arange(length + 2 * half_span, dtype=jnp.int32)[:, None]
    cols_here = jnp.arange(length, dtype=jnp.int32)[None, :]
    offset = (rows_here - cols_here - half_span).astype(jnp.float32)
    inside = jnp.abs(offset) <= half_span
    taps_axis = jnp.arange(-half_span, half_span + 1).astype(jnp.float32)
    result = []
    for spread in kernel_sigmas:
        norm_sum = jnp.sum(jnp.exp(-taps_axis * taps_axis / (2.0 * spread * spread)))
        result.append(
            jnp.where(inside, jnp.exp(-offset * offset / (2.0 * spread * spread)), 0.0) / norm_sum
        )
    return jnp.stack(result)


def local(images, mask_bits, inv_var, routes, block_slot, kernel_index, coefficients):
    peer_count = lax.axis_size("exp")
    held_count = images.shape[2]
    capacity = max(2, 2 * held_count // peer_count)
    slot_count = peer_count * capacity
    pixels = BLOCK * BLOCK
    tile_blocks = BLOCK_ROWS * BLOCK_COLS
    coef_count = coefficients.shape[0]
    usable = usable_share(mask_bits[0, 0])
    inverse = inv_var[0, 0][:, None, None]
    weight = (usable * inverse).astype(jnp.bfloat16).reshape(held_count, pixels)
    weighted = (
        (usable * inverse * images[0, 0].astype(jnp.float32))
        .astype(jnp.bfloat16)
        .reshape(held_count, pixels)
    )
    target = routes[0, 0, :, 0]
    ordinal = jnp.arange(held_count, dtype=jnp.int32)
    same_target = target[:, None] == target[None, :]
    earlier = jnp.sum(
        (same_target & (ordinal[None, :] < ordinal[:, None])).astype(jnp.int32), axis=1
    )
    position = target * capacity + earlier
    placed = jnp.arange(slot_count, dtype=jnp.int32)[:, None] == position[None, :]
    placed_int = placed.astype(jnp.int32)
    slot_block = jnp.sum(placed_int * (block_slot[0, 0] + 1)[None, :], axis=1) - 1
    slot_kernel = jnp.sum(placed_int * kernel_index[0, 0][None, :], axis=1)
    labels = jnp.stack([slot_block, slot_kernel], axis=1).reshape(peer_count, capacity, 2)
    placed_half = placed.astype(jnp.bfloat16)
    send_weight = (
        jnp.dot(placed_half, weight, preferred_element_type=jnp.float32)
        .astype(jnp.bfloat16)
        .reshape(peer_count, capacity, pixels)
    )
    block_ids = jnp.arange(tile_blocks, dtype=jnp.int32)[:, None]
    send_weighted = (
        jnp.dot(placed_half, weighted, preferred_element_type=jnp.float32)
        .astype(jnp.bfloat16)
        .reshape(peer_count, capacity, pixels)
    )
    got_weighted, got_weight, got_labels = (
        lax.all_to_all(send_weighted, "exp", split_axis=0, concat_axis=0, tiled=True),
        lax.all_to_all(send_weight, "exp", split_axis=0, concat_axis=0, tiled=True),
        lax.all_to_all(labels, "exp", split_axis=0, concat_axis=0, tiled=True),
    )
    got_labels = got_labels.reshape(slot_count, 2)
    into_block = block_ids == got_labels[:, 0][None, :]
    kernel_pick = (
        got_labels[:, 1][:, None] == jnp.arange(coef_count, dtype=jnp.int32)[None, :]
    ).astype(jnp.float32)
    slot_mix = jnp.dot(kernel_pick, coefficients, precision=lax.Precision.HIGHEST)
    mixing = slot_mix.T[:, None, :] * into_block.astype(jnp.float32)[None, :, :]
    basis_sum = jnp.einsum(
        "kbp,px->kbx",
        mixing,
        got_weighted.reshape(slot_count, pixels).astype(jnp.float32),
        precision=lax.Precision.HIGHEST,
    )
    depth_sum = jnp.dot(
        into_block.astype(jnp.bfloat16),
        got_weight.reshape(slot_count, pixels),
        preferred_element_type=jnp.float32,
    )
    tile_rows = BLOCK_ROWS * BLOCK
    tile_cols = BLOCK_COLS * BLOCK
    basis_tile = (
        basis_sum.reshape(3, BLOCK_ROWS, BLOCK_COLS, BLOCK, BLOCK)
        .transpose(0, 1, 3, 2, 4)
        .reshape(3, tile_rows, tile_cols)
    )
    depth_tile = (
        depth_sum.reshape(BLOCK_ROWS, BLOCK_COLS, BLOCK, BLOCK)
        .transpose(0, 2, 1, 3)
        .reshape(tile_rows, tile_cols)
    )
    half_span = TAPS // 2
    column_mix = band_matrix(tile_cols, half_span)
    row_mix = band_matrix(tile_rows, half_span).transpose(0, 2, 1)
    framed = extended(basis_tile, (("exp", 2), ("tile", 1)), half_span)
    across = jnp.einsum("kyp,kpc->kyc", framed, column_mix, precision=lax.Precision.HIGHEST)
    matched = jnp.einsum("kry,kyc->rc", row_mix, across, precision=lax.Precision.HIGHEST)
    denominator = 1.0 + depth_tile
    coadded = matched / denominator
    detection = lax.psum(coadded * coadded * denominator, "band")
    return (coadded[None], detection)


def solution(mesh):
    return jax.shard_map(
        local,
        mesh=mesh,
        in_specs=(
            P(("patch", "band"), "tile", "exp", None, None),
            P(("patch", "band"), "tile", "exp", None, None),
            P(("patch", "band"), "tile", "exp"),
            P(("patch", "band"), "tile", "exp", None),
            P(("patch", "band"), "tile", "exp"),
            P(("patch", "band"), "tile", "exp"),
            P(),
        ),
        out_specs=(P(("patch", "band"), "tile", "exp"), P(("patch", "tile"), "exp")),
        check_vma=False,
    )
```

profile of v0, /device:TPU:0, one launch (start us, length us, event | category | flops | bytes accessed | tf_op | source)
XLA Modules:
  0.0 137.2 jit_solution(16599511198700164798)
XLA Ops:
  7.2 0.0 copy-start
  7.2 0.0 copy-start.3
  7.2 0.7 add_bitcast_fusion
  7.9 0.9 convert_reduce_fusion
  8.8 0.7 multiply_add_fusion.1
  9.5 0.7 select_reduce_fusion.1
  10.2 0.1 stack.9
  10.3 0.1 sub.118
  10.4 0.6 copy.15
  11.0 6.3 %all-to-all-start = ((s32[4,8,2]{1,2,0:T(2,128)}), s32[4,8,2]{1,2,0:T(2,128)S(1)}, u32[]{:S(2)}, u32[]{:S(2)}) async-start(s32[4,8,2]{1,2,0:T(2,128)} %copy.15), calls=%async_computation | async-start | bytes 8192 | tf_op jit(solution)/shard_map/all_to_all | solution.py:92
  17.4 1.5 %subtract_select_fusion = f32[1,1,16,128,128]{4,3,2,1,0:T(8,128)S(1)} fusion(s32[1,1,16,128,128]{4,3,2,1,0:T(8,128)} %param.8), kind=kLoop, calls=%fused_computation.36 | loop fusion | flops 1835008 | bytes 2097152 | tf_op jit(solution)/shard_map/jit(_where)/select_n | solution.py:31
  18.8 0.0 copy-start.7
  18.8 0.0 copy-done.3
  18.8 0.1 convert.1
  18.9 0.5 copy-done.7
  19.5 2.4 %fusion = bf16[4,8,16384]{2,1,0:T(8,128)(2,1)} fusion(f32[2,8,128,128]{3,2,1,0:T(8,128)S(1)} %convert.1, f32[2,8,128,128]{3,2,1,0:T(8,128)S(1)} %bitcast.88, f32[16]{0:T(128)S(1)} %bitcast.95, s32[16]{0:T(128)S(1)} %multiply_add_fusion.1), kind=kOutput, calls=%fused_computation.2 | convolution fusion | flops 18088448 | bytes 3145856 | tf_op jit(solution)/shard_map/dot_general | solution.py:85
  21.9 1.1 all-to-all-done
  22.9 4.0 %all-to-all-start.1 = ((bf16[4,8,16384]{2,1,0:T(8,128)(2,1)}), bf16[4,8,16384]{2,1,0:T(8,128)(2,1)S(1)}, u32[]{:S(2)}, u32[]{:S(2)}) async-start(bf16[4,8,16384]{2,1,0:T(8,128)(2,1)} %fusion), calls=%async_computation.1 | async-start | bytes 2097152 | tf_op jit(solution)/shard_map/all_to_all | solution.py:90
  27.0 0.6 exponential_reduce_fusion
  27.6 0.6 exponential_reduce_fusion.1
  28.2 0.6 exponential_reduce_fusion.2
  28.8 1.8 %fusion.1 = bf16[4,8,16384]{2,1,0:T(8,128)(2,1)} fusion(f32[2,8,128,128]{3,2,1,0:T(8,128)S(1)} %bitcast.89, f32[16]{0:T(128)S(1)} %bitcast.96, s32[16]{0:T(128)S(1)} %multiply_add_fusion.1), kind=kOutput, calls=%fused_computation.3 | convolution fusion | flops 17826304 | bytes 2097280 | tf_op jit(solution)/shard_map/dot_general | solution.py:79
  30.6 2.0 %select_divide_fusion.2 = f32[1,552,512]{2,1,0:T(8,128)} fusion(f32[]{:T(128)} %exponential_reduce_fusion.2), kind=kLoop, calls=%fused_computation.26 | loop fusion | flops 2826240 | bytes 1130500 | tf_op jit(solution)/shard_map/div | solution.py:44
  32.6 3.3 %select_divide_fusion = (f32[1,552,512]{2,1,0:T(8,128)}, f32[1,552,512]{2,1,0:T(8,128)}) fusion(f32[]{:T(128)} %exponential_reduce_fusion, f32[]{:T(128)} %exponential_reduce_fusion.1), kind=kLoop, calls=%fused_computation.24 | loop fusion | flops 3674112 | bytes 2261000 | tf_op jit(solution)/shard_map/div | solution.py:44
  36.0 16.2 %all-to-all-done.1 = bf16[4,8,16384]{2,1,0:T(8,128)(2,1)S(1)} async-done(((bf16[4,8,16384]{2,1,0:T(8,128)(2,1)}), bf16[4,8,16384]{2,1,0:T(8,128)(2,1)S(1)}, u32[]{:S(2)}, u32[]{:S(2)}) %all-to-all-start.1) | async-done | bytes 1048608 | tf_op jit(solution)/shard_map/all_to_all | solution.py:90
  52.1 4.3 %all-to-all-start.2 = ((bf16[4,8,16384]{2,1,0:T(8,128)(2,1)}), bf16[4,8,16384]{2,1,0:T(8,128)(2,1)}, u32[]{:S(2)}, u32[]{:S(2)}) async-start(bf16[4,8,16384]{2,1,0:T(8,128)(2,1)} %fusion.1), calls=%async_computation.2 | async-start | bytes 2097152 | tf_op jit(solution)/shard_map/all_to_all | solution.py:91
  56.4 0.0 all-reduce.2.cloned.1.call-start
  56.4 2.2 %select_divide_fusion.3 = (f32[1,296,256]{2,1,0:T(8,128)S(1)}, f32[1,296,256]{2,1,0:T(8,128)}) fusion(f32[]{:T(128)} %exponential_reduce_fusion, f32[]{:T(128)} %exponential_reduce_fusion.1), kind=kLoop, calls=%fused_computation.48 | loop fusion | flops 985088 | bytes 606216 | tf_op jit(solution)/shard_map/div | solution.py:44
  58.6 0.1 reshape.298
  58.7 0.0 copy-done
  58.7 0.2 convolution_bitcast_fusion.2
  58.9 0.1 compare_convert_fusion
  59.0 0.3 copy.27
  59.3 1.5 %convolution_bitcast_fusion = f32[3,2,128,4,128]{4,3,2,1,0:T(4,128)S(1)} fusion(bf16[128,128,32,1,1]{1,0,2,4,3:T(8,128)(2,1)S(1)} %bitcast.91, f32[2,4,32]{2,1,0:T(4,128)S(1)} %compare_convert_fusion, f32[3,32]{1,0:T(4,128)S(1)} %convolution_bitcast_fusion.2), kind=kOutput, calls=%fused_computation.20 | convolution fusion | flops 150995712 | bytes 2622848 | tf_op jit(solution)/shard_map/kbp,px->kbx/dot_general | solution.py:101
  60.8 0.6 reshape.301
  61.4 0.2 fusion.42
  61.6 1.3 collective-permute-start.1
  62.9 4.6 %collective-permute-start = (f32[3,256,20]{2,1,0:T(8,128)S(1)}, f32[3,256,20]{2,1,0:T(8,128)S(1)}, u32[]{:S(2)}, u32[]{:S(2)}) collective-permute-start(f32[3,256,20]{2,1,0:T(8,128)S(1)} %get-tuple-element.6), channel_id=1, source_target_pairs={{0,4},{4,8},{8,12},{1,5},{5,9},{9,13},{2,6},{6,10},{10,14},{3,7},{... | collective-permute-start | bytes 184328 | tf_op jit(solution)/shard_map/ppermute | solution.py:20
  67.5 0.7 select_divide_fusion.5
  68.2 15.4 %collective-permute-done.1 = f32[3,256,20]{2,1,0:T(8,128)S(1)} collective-permute-done((f32[3,256,20]{2,1,0:T(8,128)S(1)}, f32[3,256,20]{2,1,0:T(8,128)S(1)}, u32[]{:S(2)}, u32[]{:S(2)}) %collective-permute-start.1) | collective-permute-done | bytes 61472 | tf_op jit(solution)/shard_map/ppermute | solution.py:23
  83.5 0.0 copy-start.4
  83.6 0.0 collective-permute-done
  83.6 0.0 copy-start.6
  83.6 0.9 pad_maximum_fusion.2
  84.5 0.0 copy-done.4
  84.5 0.0 copy-done.6
  84.5 0.0 copy-start.2
  84.5 1.4 %collective-permute-start.3 = (f32[3,20,552]{2,1,0:T(8,128)}, f32[3,20,552]{2,1,0:T(8,128)}, u32[]{:S(2)}, u32[]{:S(2)}) collective-permute-start(f32[3,20,552]{2,1,0:T(8,128)} %get-tuple-element.5), channel_id=1, source_target_pairs={{2,0},{3,1},{6,4},{7,5},{10,8},{11,9},{14,12},{15,13},{18,16},{19,... | collective-permute-start | bytes 397448 | tf_op jit(solution)/shard_map/ppermute | solution.py:23
  85.9 5.9 %collective-permute-start.2 = (f32[3,20,552]{2,1,0:T(8,128)S(1)}, f32[3,20,552]{2,1,0:T(8,128)}, u32[]{:S(2)}, u32[]{:S(2)}) collective-permute-start(f32[3,20,552]{2,1,0:T(8,128)S(1)} %get-tuple-element.4), channel_id=1, source_target_pairs={{0,2},{1,3},{4,6},{5,7},{8,10},{9,11},{12,14},{13,15},{16,18},{17,... | collective-permute-start | bytes 397448 | tf_op jit(solution)/shard_map/ppermute | solution.py:20
  91.8 0.0 all-to-all-done.2
  91.8 0.0 copy-start.5
  91.8 1.6 %convolution_add_fusion = f32[2,4,128,128]{3,1,2,0:T(4,128)S(1)} fusion(s32[32]{0:T(128)S(1)} %get-tuple-element.9, s32[2,4]{1,0:T(2,128)S(1)} %multiply_add_fusion, bf16[4,8,16384]{2,1,0:T(8,128)(2,1)} %all-to-all-done.2), kind=kOutput, calls=%fused_computation.22 | convolution fusion | flops 8519936 | bytes 1573024 | tf_op jit(solution)/shard_map/dot_general | solution.py:107
  93.4 0.0 collective-permute-done.3
  93.4 0.7 collective-permute-done.2
  94.1 0.0 copy-done.2
  94.2 0.0 copy-done.5
  94.2 0.0 copy-start.1
  94.2 6.7 %fusion.2 = f32[3,296,512]{2,1,0:T(8,128)S(1)} fusion(f32[1,552,512]{2,1,0:T(8,128)} %get-tuple-element.12, f32[1,552,512]{2,1,0:T(8,128)} %get-tuple-element.13, f32[1,552,512]{2,1,0:T(8,128)S(1)} %copy-done.2, f32[3,20,552]{2,1,0:T(8,128)} %collective-permute-done.3, f32[3,256,20]{2,1,0:T(8,128)S(1)} %copy-done.5, f32[3,256,512]{2,1,0:T(8,128)S(1)} %reshape.301, ...), kind=kOutput, calls=%fused_computation.4 | convolution fusion | flops 3015297792 | bytes 7170816 | tf_op jit(solution)/shard_map/kyp,kpc->kyc/dot_general | solution.py:128
  100.8 0.0 copy-done.1
  100.8 2.9 %bitcast_multiply_fusion.2 = (f32[256,512]{1,0:T(8,128)}, f32[256,512]{1,0:T(8,128)}) fusion(f32[32,8,4,128]{3,2,1,0:T(4,128)S(1)} %bitcast.92, f32[3,296,512]{2,1,0:T(8,128)S(1)} %fusion.2, f32[1,296,256]{2,1,0:T(8,128)S(1)} %get-tuple-element.14, f32[1,296,256]{2,1,0:T(8,128)S(1)} %copy-done.1, f32[1,296,256]{2,1,0:T(8,128)S(1)} %select_divide_fusion.5), kind=kOutput, calls=%fused_computation.44 | convolution fusion | flops 1397551104 | bytes 4300800 | tf_op jit(solution)/shard_map/kry,kyc->rc/dot_general | solution.py:129
  103.8 0.0 all-reduce.2.cloned.1.call-update
  103.8 24.6 %all-reduce.2.cloned.1.call-done = f32[256,512]{1,0:T(8,128)} async-done(((f32[256,512]{1,0:T(8,128)}), f32[256,512]{1,0:T(8,128)}) %all-reduce.2.cloned.1.call-update) | async-done | bytes 524304 | tf_op jit(solution)/shard_map/psum | solution.py:132
  128.4 1.9 %copy.47 = f32[256,512]{1,0:T(8,128)} copy(f32[256,512]{1,0:T(8,128)} %all-reduce.2.cloned.1.call-done) | data formatting | bytes 1048576
  (5 shorter events, 0.0 us)
Async XLA Ops:
  7.2 51.6 %copy-start = (f32[64,3]{0,1:T(4,128)S(1)}, f32[64,3]{0,1:T(4,128)}, u32[]{:S(2)}) copy-start(f32[64,3]{0,1:T(4,128)} %param.13) | copy-start | bytes 2308
  7.2 11.7 %copy-start.3 = (bf16[1,1,16,128,128]{4,3,2,1,0:T(8,128)(2,1)S(1)}, bf16[1,1,16,128,128]{4,3,2,1,0:T(8,128)(2,1)}, u32[]{:S(2)}) copy-start(bf16[1,1,16,128,128]{4,3,2,1,0:T(8,128)(2,1)} %param.7) | copy-start | bytes 1572868
  11.0 11.9 %all-to-all-start = ((s32[4,8,2]{1,2,0:T(2,128)}), s32[4,8,2]{1,2,0:T(2,128)S(1)}, u32[]{:S(2)}, u32[]{:S(2)}) async-start(s32[4,8,2]{1,2,0:T(2,128)} %copy.15), calls=%async_computation | async-start | bytes 8192 | tf_op jit(solution)/shard_map/all_to_all | solution.py:92
  18.8 0.7 copy-start.7
  22.9 29.2 %all-to-all-start.1 = ((bf16[4,8,16384]{2,1,0:T(8,128)(2,1)}), bf16[4,8,16384]{2,1,0:T(8,128)(2,1)S(1)}, u32[]{:S(2)}, u32[]{:S(2)}) async-start(bf16[4,8,16384]{2,1,0:T(8,128)(2,1)} %fusion), calls=%async_computation.1 | async-start | bytes 2097152 | tf_op jit(solution)/shard_map/all_to_all | solution.py:90
  52.1 39.7 %all-to-all-start.2 = ((bf16[4,8,16384]{2,1,0:T(8,128)(2,1)}), bf16[4,8,16384]{2,1,0:T(8,128)(2,1)}, u32[]{:S(2)}, u32[]{:S(2)}) async-start(bf16[4,8,16384]{2,1,0:T(8,128)(2,1)} %fusion.1), calls=%async_computation.2 | async-start | bytes 2097152 | tf_op jit(solution)/shard_map/all_to_all | solution.py:91
  56.4 72.0 %all-reduce.2.cloned.1.call-start = ((), (), s32[]{:S(2)}) async-start(), calls=%async_computation.3 | async-start | bytes 1048576 | tf_op jit(solution)/shard_map/psum | solution.py:132
  61.6 22.0 %collective-permute-start.1 = (f32[3,256,20]{2,1,0:T(8,128)S(1)}, f32[3,256,20]{2,1,0:T(8,128)S(1)}, u32[]{:S(2)}, u32[]{:S(2)}) collective-permute-start(f32[3,256,20]{2,1,0:T(8,128)S(1)} %get-tuple-element.7), channel_id=1, source_target_pairs={{4,0},{8,4},{12,8},{5,1},{9,5},{13,9},{6,2},{10,6},{14,10},{7,3},{... | collective-permute-start | bytes 184328 | tf_op jit(solution)/shard_map/ppermute | solution.py:23
  62.9 20.7 %collective-permute-start = (f32[3,256,20]{2,1,0:T(8,128)S(1)}, f32[3,256,20]{2,1,0:T(8,128)S(1)}, u32[]{:S(2)}, u32[]{:S(2)}) collective-permute-start(f32[3,256,20]{2,1,0:T(8,128)S(1)} %get-tuple-element.6), channel_id=1, source_target_pairs={{0,4},{4,8},{8,12},{1,5},{5,9},{9,13},{2,6},{6,10},{10,14},{3,7},{... | collective-permute-start | bytes 184328 | tf_op jit(solution)/shard_map/ppermute | solution.py:20
  83.5 0.9 copy-start.4
  83.6 0.9 copy-start.6
  84.5 9.7 %copy-start.2 = (f32[1,552,512]{2,1,0:T(8,128)S(1)}, f32[1,552,512]{2,1,0:T(8,128)}, u32[]{:S(2)}) copy-start(f32[1,552,512]{2,1,0:T(8,128)} %select_divide_fusion.2) | copy-start | bytes 3391492
  84.5 8.9 %collective-permute-start.3 = (f32[3,20,552]{2,1,0:T(8,128)}, f32[3,20,552]{2,1,0:T(8,128)}, u32[]{:S(2)}, u32[]{:S(2)}) collective-permute-start(f32[3,20,552]{2,1,0:T(8,128)} %get-tuple-element.5), channel_id=1, source_target_pairs={{2,0},{3,1},{6,4},{7,5},{10,8},{11,9},{14,12},{15,13},{18,16},{19,... | collective-permute-start | bytes 397448 | tf_op jit(solution)/shard_map/ppermute | solution.py:23
  85.9 8.2 %collective-permute-start.2 = (f32[3,20,552]{2,1,0:T(8,128)S(1)}, f32[3,20,552]{2,1,0:T(8,128)}, u32[]{:S(2)}, u32[]{:S(2)}) collective-permute-start(f32[3,20,552]{2,1,0:T(8,128)S(1)} %get-tuple-element.4), channel_id=1, source_target_pairs={{0,2},{1,3},{4,6},{5,7},{8,10},{9,11},{12,14},{13,15},{16,18},{17,... | collective-permute-start | bytes 397448 | tf_op jit(solution)/shard_map/ppermute | solution.py:20
  91.8 2.4 %copy-start.5 = (f32[3,256,20]{2,1,0:T(8,128)S(1)}, f32[3,256,20]{2,1,0:T(8,128)}, u32[]{:S(2)}) copy-start(f32[3,256,20]{2,1,0:T(8,128)} %copy-done.4) | copy-start | bytes 184324
  94.2 6.7 %copy-start.1 = (f32[1,296,256]{2,1,0:T(8,128)S(1)}, f32[1,296,256]{2,1,0:T(8,128)}, u32[]{:S(2)}) copy-start(f32[1,296,256]{2,1,0:T(8,128)} %get-tuple-element.15) | copy-start | bytes 909316
Sparse Core Ops, SparseCore 0:
  103.9 24.4 all-reduce.1
where the time goes:
time: 138 us; the launch traced here: 137 us
  waiting for transfers between devices  58 us (42%)
  starting transfers between devices  27.8 us (20%)
  matrix products  17 us (12%)
  other arithmetic  15.7 us (11%)
  between operations  14.2 us (10%)
  local copies, waits for them, and re-layouts  4.37 us (3%)
    psum x1, waiting for transfers between devices, local(): detection = lax.psum(coadded * coadded * denominator, 'band')  24.6 us
    all_to_all x1, waiting for transfers between devices, local(): lax.all_to_all(send_weighted, 'exp', split_axis=0, concat_axis=0, tiled=T...  16.2 us
    ppermute x2, waiting for transfers between devices, extended(): lax.ppermute(lax.slice_in_dim(block, 0, width, axis=dim), axis, backward)  15.4 us
    ppermute x2, starting transfers between devices, extended(): lax.ppermute(lax.slice_in_dim(block, block.shape[dim] - width, None, axis...  10.5 us
    div x4, other arithmetic, band_matrix(): jnp.where(inside, jnp.exp(-offset * offset / (2.0 * spread * spread)), 0.0)  8.28 us
    dot_general x1, matrix products, local(): jnp.einsum('kyp,kpc->kyc', framed, column_mix, precision=lax.Precision.HI...  6.67 us
    all_to_all x1, starting transfers between devices, local(): lax.all_to_all(labels, 'exp', split_axis=0, concat_axis=0, tiled=True)  6.35 us
    all_to_all x1, starting transfers between devices, local(): lax.all_to_all(send_weight, 'exp', split_axis=0, concat_axis=0, tiled=True)  4.26 us
  transfers between devices with their start and end apart: 8, of which 5 were waited for; matrix products, arithmetic and copies ran while one was open for 16% of the time, Pallas kernels for 0%

commit v1 on v0

v1 whole, which is shorter than its diff:
```python
import functools

import jax
import jax.numpy as jnp
import numpy as np
from jax import lax
from jax.experimental import pallas as pl
from jax.experimental.pallas import tpu as pltpu
from jax.sharding import PartitionSpec as P

BLOCK = 128
TAPS = 41
BLOCK_ROWS = 2
BLOCK_COLS = 4
SPILL = 32

kernel_sigmas = (1.0, 2.5, 6.0)
MESH = pl.DeviceIdType.MESH


def tap_matrix(rows, cols, shift):
    half_span = TAPS // 2
    offset = np.arange(rows)[:, None] - np.arange(cols)[None, :] - shift
    axis = np.arange(-half_span, half_span + 1).astype(np.float64)
    result = []
    for spread in kernel_sigmas:
        norm = np.sum(np.exp(-axis * axis / (2.0 * spread * spread)))
        result.append(
            np.where(
                np.abs(offset) <= half_span,
                np.exp(-offset * offset / (2.0 * spread * spread)),
                0.0,
            )
            / norm
        )
    return np.stack(result)


def tap_pair(taps):
    high = taps.astype(jnp.bfloat16)
    low = (taps - high.astype(np.float64)).astype(jnp.bfloat16)
    return jnp.asarray(np.stack([high, low]))


def split(value):
    high = value.astype(jnp.bfloat16)
    return high, (value - high.astype(jnp.float32)).astype(jnp.bfloat16)


def dot3(left, right):
    (left_high, left_low), (right_high, right_low) = left, right
    dot = functools.partial(jnp.dot, preferred_element_type=jnp.float32)
    return dot(left_high, right_high) + (dot(left_high, right_low) + dot(left_low, right_high))


def place_kernel(
    n, held, me, routes, slots, kernels, inverse, coefs, images, masks, across, down,
    depth, matched, own, spill_up, spill_down, acc, wide,
):
    blocks = BLOCK_ROWS * BLOCK_COLS
    tile_rows = BLOCK_ROWS * BLOCK
    tile_cols = BLOCK_COLS * BLOCK
    half = tile_cols // 2
    wide[...] = jnp.zeros_like(wide)

    def place(d, carry):
        acc[...] = jnp.zeros_like(acc)

        def one(i, carry):
            @pl.when(routes[i] == d)
            def _():
                slot = slots[i]
                which = kernels[i]
                row = slot // BLOCK_COLS
                col = slot % BLOCK_COLS
                rows = pl.ds(pl.multiple_of(row * BLOCK, BLOCK), BLOCK)
                cols = pl.ds(pl.multiple_of(col * BLOCK, BLOCK), BLOCK)
                bits = masks[i]
                suspect = jnp.bitwise_and(bits, 1).astype(jnp.float32)
                usable = jnp.where(
                    jnp.bitwise_and(bits, 6) == 6, 0.0, 1.0 - 0.5 * suspect
                )
                scaled = usable * inverse[i]
                weighted = (
                    (scaled * images[i].astype(jnp.float32))
                    .astype(jnp.bfloat16)
                    .astype(jnp.float32)
                )
                weight = scaled.astype(jnp.bfloat16).astype(jnp.float32)
                for k in range(3):
                    acc[k, rows, cols] += coefs[which, k] * weighted
                acc[3, rows, cols] += weight

            return carry

        lax.fori_loop(0, held, one, 0)
        depth[d] = acc[3].astype(jnp.bfloat16)
        highs, lows = [], []
        for k in range(3):
            tall = dot3((down[0, k], down[1, k]), split(acc[k]))
            high, low = split(tall)
            highs.append(high)
            lows.append(low)
        base = d * tile_cols
        for piece in range(3):
            left = max(0, piece - 1) * half
            right = min(2, piece + 1) * half
            top = left - (piece - 1) * half
            total = None
            for k in range(3):
                term = dot3(
                    (highs[k][:, left:right], lows[k][:, left:right]),
                    (
                        across[0, k, top : top + right - left],
                        across[1, k, top : top + right - left],
                    ),
                )
                total = term if total is None else total + term
            start = pl.multiple_of(base + piece * half, BLOCK)
            wide[:, pl.ds(start, half)] += total
        return carry

    lax.fori_loop(0, n, place, 0)

    def emit(d, carry):
        start = pl.multiple_of(BLOCK + d * tile_cols, BLOCK)
        cols = pl.ds(start, tile_cols)
        matched[d] = wide[SPILL : SPILL + tile_rows, cols].astype(jnp.bfloat16)
        spill_up[d] = wide[0:SPILL, cols].astype(jnp.bfloat16)
        spill_down[d] = wide[SPILL + tile_rows :, cols].astype(jnp.bfloat16)
        return carry

    lax.fori_loop(0, n, emit, 0)
    start = pl.multiple_of(BLOCK + me[0] * tile_cols, BLOCK)
    own[...] = wide[SPILL : SPILL + tile_rows, pl.ds(start, tile_cols)]


def reduce_kernel(
    n, strips, bands, depth, matched, own, spill_up, spill_down, coadd, detection,
    moving, outgoing, incoming, spilled, det_mine, det_theirs,
    send_sem, recv_sem, match_send, match_recv,
    spill_send, spill_recv, det_send, det_recv,
):
    me = lax.axis_index("exp")
    strip = lax.axis_index("tile")
    band = lax.axis_index("band")
    rows_all = depth.shape[1]
    chunk = 32
    barrier = pltpu.get_barrier_semaphore()
    greet = [
        (strip > 0, {"tile": strip - 1}),
        (strip < strips - 1, {"tile": strip + 1}),
    ]
    for here, peer in greet:

        @pl.when(here)
        def _(peer=peer):
            pl.semaphore_signal(barrier, inc=1, device_id=peer, device_id_type=MESH)

    for j in range(1, n):
        pl.semaphore_signal(
            barrier, inc=1, device_id={"exp": lax.rem(me + j, n)}, device_id_type=MESH
        )
    for j in range(1, bands):
        pl.semaphore_signal(
            barrier, inc=1, device_id={"band": lax.rem(band + j, bands)}, device_id_type=MESH
        )
    peers = bands - 1 + n - 1
    for here, _peer in greet:
        peers = peers + here.astype(jnp.int32)
    pl.semaphore_wait(barrier, peers)

    def spill_copy(side):
        peer = strip + 1 if side == 0 else strip - 1
        return pltpu.make_async_remote_copy(
            src_ref=spill_down if side == 0 else spill_up,
            dst_ref=spilled.at[side],
            send_sem=spill_send.at[side],
            recv_sem=spill_recv.at[side],
            device_id={"tile": peer},
            device_id_type=MESH,
        )

    sends_spill = (strip < strips - 1, strip > 0)
    gets_spill = (strip > 0, strip < strips - 1)
    for side in range(2):

        @pl.when(sends_spill[side])
        def _(side=side):
            spill_copy(side).start()

        @pl.when(jnp.logical_not(gets_spill[side]))
        def _(side=side):
            spilled[side] = jnp.zeros(spilled.shape[1:], spilled.dtype)

    def unit_copy(d, right):
        place = d if right else jnp.where(d == me - 1, n, d)
        return pltpu.make_async_remote_copy(
            src_ref=moving.at[d],
            dst_ref=moving.at[place],
            send_sem=send_sem.at[d],
            recv_sem=recv_sem.at[place],
            device_id={"exp": me + 1 if right else me - 1},
            device_id_type=MESH,
        )

    def arrived(place):
        pltpu.make_async_remote_copy(
            src_ref=moving.at[place],
            dst_ref=moving.at[place],
            send_sem=send_sem.at[0],
            recv_sem=recv_sem.at[place],
            device_id={"band": lax.rem(band + 1, bands)},
            device_id_type=MESH,
        ).wait_recv()

    def pass_on(d, right, gets):
        @pl.when(gets)
        def _():
            arrived(d)
            for r in range(0, rows_all, chunk):
                rows = slice(r, r + chunk)
                moving[d, rows] = (
                    moving[d, rows].astype(jnp.float32) + depth[d, rows].astype(jnp.float32)
                ).astype(jnp.bfloat16)

        @pl.when(jnp.logical_not(gets))
        def _():
            for r in range(0, rows_all, chunk):
                moving[d, r : r + chunk] = depth[d, r : r + chunk]

        unit_copy(d, right).start()

    def match_copy(j):
        return pltpu.make_async_remote_copy(
            src_ref=outgoing.at[j],
            dst_ref=incoming.at[j],
            send_sem=match_send.at[j],
            recv_sem=match_recv.at[j],
            device_id={"exp": lax.rem(me + j, n)},
            device_id_type=MESH,
        )

    def edges(d, r):
        value = None
        if r < SPILL:
            value = spilled[0, d, r : r + chunk].astype(jnp.float32)
        if r >= rows_all - SPILL:
            low = r - (rows_all - SPILL)
            value = spilled[1, d, low : low + chunk].astype(jnp.float32)
        return value

    def step_depth(gets_now):
        def step(s, carry):
            to_right = n - 1 - s

            @pl.when((to_right > me) & ((me > 0) == gets_now))
            def _():
                pass_on(to_right, True, me > 0)

            @pl.when((s < me) & ((me < n - 1) == gets_now))
            def _():
                pass_on(s, False, me < n - 1)

            return carry

        lax.fori_loop(0, n - 1, step, 0)

    step_depth(False)
    for side in range(2):

        @pl.when(gets_spill[side])
        def _(side=side):
            spill_copy(side).wait_recv()

    def send_match(i, carry):
        j = n - 1 - i
        d = lax.rem(me + j, n)
        for r in range(0, rows_all, chunk):
            rows = slice(r, r + chunk)
            edge = edges(d, r)
            if edge is None:
                outgoing[j, rows] = matched[d, rows]
            else:
                outgoing[j, rows] = (matched[d, rows].astype(jnp.float32) + edge).astype(
                    jnp.bfloat16
                )
        match_copy(j).start()
        return carry

    lax.fori_loop(0, n - 1, send_match, 0)
    step_depth(True)

    @pl.when(me > 0)
    def _():
        arrived(me)

    @pl.when(me == 0)
    def _():
        moving[me] = jnp.zeros(moving.shape[1:], moving.dtype)

    @pl.when(me < n - 1)
    def _():
        arrived(n)

    @pl.when(me == n - 1)
    def _():
        moving[n] = jnp.zeros(moving.shape[1:], moving.dtype)

    for r in range(0, rows_all, chunk):
        rows = slice(r, r + chunk)
        edge = edges(me, r)
        coadd[rows] = own[rows] if edge is None else own[rows] + edge

    def gather(i, carry):
        j = i + 1
        match_copy(j).wait_recv()
        for r in range(0, rows_all, chunk):
            rows = slice(r, r + chunk)
            coadd[rows] += incoming[j, rows].astype(jnp.float32)
        return carry

    lax.fori_loop(0, n - 1, gather, 0)
    for r in range(0, rows_all, chunk):
        rows = slice(r, r + chunk)
        denominator = 1.0 + (
            depth[me, rows].astype(jnp.float32)
            + moving[me, rows].astype(jnp.float32)
            + moving[n, rows].astype(jnp.float32)
        )
        value = coadd[rows] / denominator
        coadd[rows] = value
        det_mine[rows] = value * value * denominator

    def det_copy(j):
        return pltpu.make_async_remote_copy(
            src_ref=det_mine,
            dst_ref=det_theirs.at[j - 1],
            send_sem=det_send.at[j - 1],
            recv_sem=det_recv.at[j - 1],
            device_id={"band": lax.rem(band + j, bands)},
            device_id_type=MESH,
        )

    for j in range(1, bands):
        det_copy(j).start()
    for j in range(1, bands):
        det_copy(j).wait()
    for r in range(0, rows_all, chunk):
        rows = slice(r, r + chunk)
        value = det_mine[rows]
        for j in range(1, bands):
            value += det_theirs[j - 1, rows]
        detection[rows] = value

    def drain(s, carry):
        to_right = n - 1 - s
        match_copy(s + 1).wait_send()

        @pl.when(to_right > me)
        def _():
            unit_copy(to_right, True).wait_send()

        @pl.when(s < me)
        def _():
            unit_copy(s, False).wait_send()

        return carry

    lax.fori_loop(0, n - 1, drain, 0)
    for side in range(2):

        @pl.when(sends_spill[side])
        def _(side=side):
            spill_copy(side).wait_send()


def local(sizes, images, mask_bits, inv_var, routes, block_slot, kernel_index, coefficients):
    n, strips, bands = sizes["exp"], sizes["tile"], sizes["band"]
    held = images.shape[2]
    tile_rows = BLOCK_ROWS * BLOCK
    tile_cols = BLOCK_COLS * BLOCK
    half = tile_cols // 2
    across = tap_pair(tap_matrix(2 * half, half, BLOCK))
    down = tap_pair(tap_matrix(tile_rows + 2 * SPILL, tile_rows, SPILL))
    smem = pl.BlockSpec(memory_space=pltpu.SMEM)
    vmem = pl.BlockSpec(memory_space=pltpu.VMEM)
    plane = jax.ShapeDtypeStruct((n, tile_rows, tile_cols), jnp.bfloat16)
    spill = jax.ShapeDtypeStruct((n, SPILL, tile_cols), jnp.bfloat16)
    whole = jax.ShapeDtypeStruct((tile_rows, tile_cols), jnp.float32)
    placed = pl.pallas_call(
        functools.partial(place_kernel, n, held),
        out_shape=(plane, plane, whole, spill, spill),
        in_specs=[smem] * 6 + [vmem] * 4,
        out_specs=(vmem,) * 5,
        scratch_shapes=[
            pltpu.VMEM((4, tile_rows, tile_cols), jnp.float32),
            pltpu.VMEM((tile_rows + 2 * SPILL, n * tile_cols + 2 * BLOCK), jnp.float32),
        ],
        name="place_and_match",
    )(
        lax.axis_index("exp").reshape(1), routes[0, 0, :, 0], block_slot[0, 0],
        kernel_index[0, 0], inv_var[0, 0], coefficients, images[0, 0], mask_bits[0, 0],
        across, down,
    )
    coadd, detection = pl.pallas_call(
        functools.partial(reduce_kernel, n, strips, bands),
        out_shape=(whole, whole),
        in_specs=[vmem] * 5,
        out_specs=(vmem, vmem),
        scratch_shapes=[
            pltpu.VMEM((n + 1, tile_rows, tile_cols), jnp.bfloat16),
            pltpu.VMEM((n, tile_rows, tile_cols), jnp.bfloat16),
            pltpu.VMEM((n, tile_rows, tile_cols), jnp.bfloat16),
            pltpu.VMEM((2, n, SPILL, tile_cols), jnp.bfloat16),
            pltpu.VMEM((tile_rows, tile_cols), jnp.float32),
            pltpu.VMEM((bands - 1, tile_rows, tile_cols), jnp.float32),
            pltpu.SemaphoreType.DMA((n,)),
            pltpu.SemaphoreType.DMA((n + 1,)),
            pltpu.SemaphoreType.DMA((n,)),
            pltpu.SemaphoreType.DMA((n,)),
            pltpu.SemaphoreType.DMA((2,)),
            pltpu.SemaphoreType.DMA((2,)),
            pltpu.SemaphoreType.DMA((bands - 1,)),
            pltpu.SemaphoreType.DMA((bands - 1,)),
        ],
        compiler_params=pltpu.CompilerParams(collective_id=0, has_side_effects=True),
        name="reduce_and_finish",
    )(*placed)
    return coadd[None], detection


def solution(mesh):
    return jax.shard_map(
        functools.partial(local, dict(mesh.shape)),
        mesh=mesh,
        in_specs=(
            P(("patch", "band"), "tile", "exp", None, None),
            P(("patch", "band"), "tile", "exp", None, None),
            P(("patch", "band"), "tile", "exp"),
            P(("patch", "band"), "tile", "exp", None),
            P(("patch", "band"), "tile", "exp"),
            P(("patch", "band"), "tile", "exp"),
            P(),
        ),
        out_specs=(P(("patch", "band"), "tile", "exp"), P(("patch", "tile"), "exp")),
        check_vma=False,
    )
```

time: 138 us -> 80 us (0.58)
  Pallas kernels: 0 us -> 74 us
  waiting for transfers between devices: 58 us -> 0 us
  starting transfers between devices: 27.8 us -> 0 us
  matrix products: 17 us -> 0 us
  other arithmetic: 15.7 us -> 0 us
  between operations: 14.2 us -> 0.64 us
    pallas_call x0 -> x2, Pallas kernels: none -> 74 us  [the longest x1 57.6 us: local(): pl.pallas_call(functools.partial(reduce_kernel, n, strips, bands), out_sh...]
    psum x1 -> x0, waiting for transfers between devices: 24.6 us -> none  [local(): detection = lax.psum(coadded * coadded * denominator, 'band')]
    all_to_all x3 -> x0, waiting for transfers between devices: 17.2 us -> none  [the longest x1 16.2 us: local(): lax.all_to_all(send_weighted, 'exp', split_axis=0, concat_axis=0, tiled=T...]
    dot_general x7 -> x0, matrix products: 17 us -> none  [the longest x1 6.67 us: local(): jnp.einsum('kyp,kpc->kyc', framed, column_mix, precision=lax.Precision.HI...]
    ppermute x4 -> x0, waiting for transfers between devices: 16.1 us -> none  [the longest x2 15.4 us: extended(): lax.ppermute(lax.slice_in_dim(block, 0, width, axis=dim), axis, backward)]
    all_to_all x3 -> x0, starting transfers between devices: 14.6 us -> none  [the longest x1 6.35 us: local(): lax.all_to_all(labels, 'exp', split_axis=0, concat_axis=0, tiled=True)]
    ppermute x4 -> x0, starting transfers between devices: 13.2 us -> none  [the longest x2 10.5 us: extended(): lax.ppermute(lax.slice_in_dim(block, block.shape[dim] - width, None, axis...]
    div x4 -> x0, other arithmetic: 8.28 us -> none  [band_matrix(): jnp.where(inside, jnp.exp(-offset * offset / (2.0 * spread * spread)), 0.0)]
  transfers between devices with their start and end apart: 8 -> 0, of which waited for: 5 -> 0; matrix products, arithmetic and copies ran while one was open for 16% -> 0% of each run, Pallas kernels for 0% -> 0%
where the time goes in v1:
time: 80 us; the launch traced here: 79.7 us
  Pallas kernels  74 us (92%)
  local copies, waits for them, and re-layouts  5.11 us (6%)
    pallas_call x1, Pallas kernels, local(): pl.pallas_call(functools.partial(reduce_kernel, n, strips, bands), out_sh...  57.6 us
    pallas_call x1, Pallas kernels, local(): pl.pallas_call(functools.partial(place_kernel, n, held), out_shape=(plane...  16.3 us
    unnamed x3, local copies, waits for them, and re-layouts  5.11 us

profile of v1, /device:TPU:0, one launch (start us, length us, event | category | flops | bytes accessed | tf_op | source)
XLA Modules:
  0.0 79.7 jit_solution(13105227872224185937)
XLA Ops:
  0.6 1.4 %copy.11.coefs = f32[64,3]{1,0:T(8,128)} copy(f32[64,3]{0,1:T(4,128)} %param.15) | data formatting | bytes 1536 | tf_op args[6]
  2.0 16.3 %place_and_match.1 = (bf16[4,256,512]{2,1,0:T(8,128)(2,1)}, bf16[4,256,512]{2,1,0:T(8,128)(2,1)}, f32[256,512]{1,0:T(8,128)}, bf16[4,32,512]{2,1,0:T(8,128)(2,1)}, bf16[4,32,512]{2,1,0:T(8,128)(2,1)}) custom-call(s32[1]{0:T(128)} %bitcast.me, s32[16]{0:T(128)} %bitcast.11, s32[16]{0:T(128)} %bitcast.12, s32[16]{0:T(128)} %bitcast.13, f32[16]{0:T(128)} %bitcast.14, ...), custom_call_target="tpu_custom_call" | custom-call | tf_op jit(solution)/shard_map/place_and_match/pallas_call | solution.py:391
  18.3 57.6 %reduce_and_finish.1 = (f32[256,512]{1,0:T(8,128)}, f32[256,512]{1,0:T(8,128)}) custom-call(bf16[4,256,512]{2,1,0:T(8,128)(2,1)} %get-tuple-element.9.depth, bf16[4,256,512]{2,1,0:T(8,128)(2,1)} %get-tuple-element.10.matched, f32[256,512]{1,0:T(8,128)} %get-tuple-element.11.own, bf16[4,32,512]{2,1,0:T(8,128)(2,1)} %get-tuple-element.12.spill_up, ...), custom_call_target="tpu_custom_call" | custom-call | tf_op jit(solution)/shard_map/reduce_and_finish/pallas_call | solution.py:406
  76.0 1.9 %copy.14 = f32[1,256,512]{2,1,0:T(8,128)} copy(f32[1,256,512]{2,1,0:T(8,128)} %bitcast.9) | data formatting | bytes 1048576
  77.8 1.9 %copy.15 = f32[256,512]{1,0:T(8,128)} copy(f32[256,512]{1,0:T(8,128)} %get-tuple-element.19) | data formatting | bytes 1048576

commit v2 on v1

v2 whole, which is shorter than its diff:
```python
import functools

import jax
import jax.numpy as jnp
import numpy as np
from jax import lax
from jax.experimental import pallas as pl
from jax.experimental.pallas import tpu as pltpu
from jax.sharding import PartitionSpec as P

BLOCK = 128
TAPS = 41
BLOCK_ROWS = 2
BLOCK_COLS = 4
SPILL = 32

kernel_sigmas = (1.0, 2.5, 6.0)
MESH = pl.DeviceIdType.MESH


def tap_matrix(rows, cols, shift):
    half_span = TAPS // 2
    offset = np.arange(rows)[:, None] - np.arange(cols)[None, :] - shift
    axis = np.arange(-half_span, half_span + 1).astype(np.float64)
    result = []
    for spread in kernel_sigmas:
        norm = np.sum(np.exp(-axis * axis / (2.0 * spread * spread)))
        result.append(
            np.where(
                np.abs(offset) <= half_span,
                np.exp(-offset * offset / (2.0 * spread * spread)),
                0.0,
            )
            / norm
        )
    return np.stack(result)


def tap_pair(taps):
    high = taps.astype(jnp.bfloat16)
    low = (taps - high.astype(np.float64)).astype(jnp.bfloat16)
    return jnp.asarray(np.stack([high, low]))


def split(value):
    high = value.astype(jnp.bfloat16)
    return high, (value - high.astype(jnp.float32)).astype(jnp.bfloat16)


def dot3(left, right):
    (left_high, left_low), (right_high, right_low) = left, right
    dot = functools.partial(jnp.dot, preferred_element_type=jnp.float32)
    return dot(left_high, right_high) + (dot(left_high, right_low) + dot(left_low, right_high))


def place_kernel(
    held, routes, slots, kernels, inverse, coefs, images, masks, depth, basis, acc
):
    d = pl.program_id(0)
    acc[...] = jnp.zeros_like(acc)

    def one(i, carry):
        @pl.when(routes[i] == d)
        def _():
            slot = slots[i]
            which = kernels[i]
            rows = pl.ds(pl.multiple_of(slot // BLOCK_COLS * BLOCK, BLOCK), BLOCK)
            cols = pl.ds(pl.multiple_of(slot % BLOCK_COLS * BLOCK, BLOCK), BLOCK)
            bits = masks[i]
            suspect = jnp.bitwise_and(bits, 1).astype(jnp.float32)
            usable = jnp.where(jnp.bitwise_and(bits, 6) == 6, 0.0, 1.0 - 0.5 * suspect)
            scaled = usable * inverse[i]
            weighted = (
                (scaled * images[i].astype(jnp.float32)).astype(jnp.bfloat16).astype(jnp.float32)
            )
            weight = scaled.astype(jnp.bfloat16).astype(jnp.float32)
            for k in range(3):
                acc[k, rows, cols] += coefs[k, which] * weighted
            acc[3, rows, cols] += weight

        return carry

    lax.fori_loop(0, held, one, 0)
    depth[0] = acc[3].astype(jnp.bfloat16)
    for k in range(3):
        basis[0, 0, k], basis[0, 1, k] = split(acc[k])


def reduce_kernel(
    n, strips, bands, depth, basis, across, down, numerator, denominator, det_mine, det_theirs,
    moving, outgoing, incoming, framed, result, spilling, spilled,
    send_sem, recv_sem, match_send, match_recv,
    spill_send, spill_recv, det_send, det_recv, frame_sem,
):
    me = lax.axis_index("exp")
    strip = lax.axis_index("tile")
    band = lax.axis_index("band")
    rows_all = depth.shape[1]
    chunk = 32
    barrier = pltpu.get_barrier_semaphore()
    greet = [
        (strip > 0, {"tile": strip - 1}),
        (strip < strips - 1, {"tile": strip + 1}),
    ]
    for here, peer in greet:

        @pl.when(here)
        def _(peer=peer):
            pl.semaphore_signal(barrier, inc=1, device_id=peer, device_id_type=MESH)

    for j in range(1, n):
        pl.semaphore_signal(
            barrier, inc=1, device_id={"exp": lax.rem(me + j, n)}, device_id_type=MESH
        )
    for j in range(1, bands):
        pl.semaphore_signal(
            barrier, inc=1, device_id={"band": lax.rem(band + j, bands)}, device_id_type=MESH
        )
    peers = bands - 1 + n - 1
    for here, _peer in greet:
        peers = peers + here.astype(jnp.int32)
    pl.semaphore_wait(barrier, peers)

    tile_cols = depth.shape[2]
    half = tile_cols // 2

    def frame_copies(j, slot):
        d = lax.rem(me + j, n)
        before = jnp.maximum(d - 1, 0)
        after = jnp.minimum(d + 1, n - 1)
        whole = pl.ds(BLOCK, tile_cols)
        return (
            pltpu.make_async_copy(
                basis.at[d], framed.at[slot, :, :, :, whole], frame_sem.at[slot, 0]
            ),
            pltpu.make_async_copy(
                basis.at[before, :, :, :, pl.ds(tile_cols - BLOCK, BLOCK)],
                framed.at[slot, :, :, :, pl.ds(0, BLOCK)],
                frame_sem.at[slot, 1],
            ),
            pltpu.make_async_copy(
                basis.at[after, :, :, :, pl.ds(0, BLOCK)],
                framed.at[slot, :, :, :, pl.ds(BLOCK + tile_cols, BLOCK)],
                frame_sem.at[slot, 2],
            ),
        )

    def spill_copy(side, j):
        peer = strip + 1 if side == 0 else strip - 1
        return pltpu.make_async_remote_copy(
            src_ref=spilling.at[side, j],
            dst_ref=spilled.at[side, j],
            send_sem=spill_send.at[side, j],
            recv_sem=spill_recv.at[side, j],
            device_id={"tile": peer},
            device_id_type=MESH,
        )

    sends_spill = (strip < strips - 1, strip > 0)
    gets_spill = (strip > 0, strip < strips - 1)
    for side in range(2):

        @pl.when(jnp.logical_not(gets_spill[side]))
        def _(side=side):
            spilled[side] = jnp.zeros(spilled.shape[1:], spilled.dtype)

    def correlate(j, slot):
        d = lax.rem(me + j, n)
        for copy in frame_copies(j, slot):
            copy.wait()

        @pl.when(d == 0)
        def _():
            framed[slot, :, :, :, 0:BLOCK] = jnp.zeros(
                framed.shape[1:4] + (BLOCK,), framed.dtype
            )

        @pl.when(d == n - 1)
        def _():
            framed[slot, :, :, :, BLOCK + tile_cols :] = jnp.zeros(
                framed.shape[1:4] + (BLOCK,), framed.dtype
            )

        for h in range(2):
            total = None
            for k in range(3):
                cols = slice(h * half, h * half + half + 2 * BLOCK)
                tall = dot3(
                    (down[0, k], down[1, k]),
                    (framed[slot, 0, k, :, cols], framed[slot, 1, k, :, cols]),
                )
                term = dot3(split(tall), (across[0, k], across[1, k]))
                total = term if total is None else total + term
            out = slice(h * half, (h + 1) * half)
            result[slot, :, out] = total[SPILL : SPILL + rows_all]
            spilling[0, j, :, out] = total[SPILL + rows_all :].astype(jnp.bfloat16)
            spilling[1, j, :, out] = total[0:SPILL].astype(jnp.bfloat16)
        for side in range(2):

            @pl.when(sends_spill[side])
            def _(side=side):
                spill_copy(side, j).start()

    def unit_copy(d, right):
        place = d if right else jnp.where(d == me - 1, n, d)
        return pltpu.make_async_remote_copy(
            src_ref=moving.at[d],
            dst_ref=moving.at[place],
            send_sem=send_sem.at[d],
            recv_sem=recv_sem.at[place],
            device_id={"exp": me + 1 if right else me - 1},
            device_id_type=MESH,
        )

    def arrived(place):
        pltpu.make_async_remote_copy(
            src_ref=moving.at[place],
            dst_ref=moving.at[place],
            send_sem=send_sem.at[0],
            recv_sem=recv_sem.at[place],
            device_id={"band": lax.rem(band + 1, bands)},
            device_id_type=MESH,
        ).wait_recv()

    def pass_on(d, right, gets):
        @pl.when(gets)
        def _():
            arrived(d)
            for r in range(0, rows_all, chunk):
                rows = slice(r, r + chunk)
                moving[d, rows] = (
                    moving[d, rows].astype(jnp.float32) + depth[d, rows].astype(jnp.float32)
                ).astype(jnp.bfloat16)

        @pl.when(jnp.logical_not(gets))
        def _():
            for r in range(0, rows_all, chunk):
                moving[d, r : r + chunk] = depth[d, r : r + chunk]

        unit_copy(d, right).start()

    def match_copy(j):
        return pltpu.make_async_remote_copy(
            src_ref=outgoing.at[j],
            dst_ref=incoming.at[j],
            send_sem=match_send.at[j],
            recv_sem=match_recv.at[j],
            device_id={"exp": lax.rem(me + j, n)},
            device_id_type=MESH,
        )

    def edges(j, r):
        value = None
        if r < SPILL:
            value = spilled[0, j, r : r + chunk].astype(jnp.float32)
        if r >= rows_all - SPILL:
            low = r - (rows_all - SPILL)
            value = spilled[1, j, low : low + chunk].astype(jnp.float32)
        return value

    def complete(j, slot):
        for side in range(2):

            @pl.when(gets_spill[side])
            def _(side=side):
                spill_copy(side, j).wait_recv()

        for r in range(0, rows_all, chunk):
            rows = slice(r, r + chunk)
            edge = edges(j, r)
            value = result[slot, rows]
            if edge is not None:
                value += edge
            if isinstance(j, int):
                numerator[rows] = value
            else:
                outgoing[j, rows] = value.astype(jnp.bfloat16)

    def step_right(s, carry):
        @pl.when(n - 1 - s > me)
        def _():
            pass_on(n - 1 - s, True, me > 0)

        return carry

    def step_left(s, carry):
        @pl.when(s < me)
        def _():
            pass_on(s, False, me < n - 1)

        return carry

    for copy in frame_copies(n - 1, 0):
        copy.start()

    @pl.when(me == 0)
    def _():
        lax.fori_loop(0, n - 1, step_right, 0)

    @pl.when(me == n - 1)
    def _():
        lax.fori_loop(0, n - 1, step_left, 0)

    def turn(i, carry):
        j = n - 1 - i
        slot = lax.rem(i, 2)

        @pl.when(i < n - 1)
        def _():
            for copy in frame_copies(j - 1, 1 - slot):
                copy.start()

        correlate(j, slot)

        @pl.when(i > 0)
        def _():
            complete(j + 1, 1 - slot)
            match_copy(j + 1).start()

        return carry

    lax.fori_loop(0, n, turn, 0)
    complete(0, (n - 1) % 2)

    right_first = 2 * me < n - 1

    @pl.when(right_first & (me > 0))
    def _():
        lax.fori_loop(0, n - 1, step_right, 0)

    @pl.when(me < n - 1)
    def _():
        lax.fori_loop(0, n - 1, step_left, 0)

    @pl.when(jnp.logical_not(right_first) & (me > 0))
    def _():
        lax.fori_loop(0, n - 1, step_right, 0)

    @pl.when(me > 0)
    def _():
        arrived(me)

    @pl.when(me == 0)
    def _():
        moving[me] = jnp.zeros(moving.shape[1:], moving.dtype)

    @pl.when(me < n - 1)
    def _():
        arrived(n)

    @pl.when(me == n - 1)
    def _():
        moving[n] = jnp.zeros(moving.shape[1:], moving.dtype)

    def gather(i, carry):
        j = i + 1
        match_copy(j).wait_recv()
        for r in range(0, rows_all, chunk):
            rows = slice(r, r + chunk)
            numerator[rows] += incoming[j, rows].astype(jnp.float32)
        return carry

    lax.fori_loop(0, n - 1, gather, 0)
    for r in range(0, rows_all, chunk):
        rows = slice(r, r + chunk)
        below = 1.0 + (
            depth[me, rows].astype(jnp.float32)
            + moving[me, rows].astype(jnp.float32)
            + moving[n, rows].astype(jnp.float32)
        )
        denominator[rows] = below
        value = numerator[rows] / below
        det_mine[rows] = value * value * below

    def det_copy(j):
        return pltpu.make_async_remote_copy(
            src_ref=det_mine,
            dst_ref=det_theirs.at[j - 1],
            send_sem=det_send.at[j - 1],
            recv_sem=det_recv.at[j - 1],
            device_id={"band": lax.rem(band + j, bands)},
            device_id_type=MESH,
        )

    for j in range(1, bands):
        det_copy(j).start()
    for j in range(1, bands):
        det_copy(j).wait()

    def drain(s, carry):
        to_right = n - 1 - s
        match_copy(s + 1).wait_send()

        @pl.when(to_right > me)
        def _():
            unit_copy(to_right, True).wait_send()

        @pl.when(s < me)
        def _():
            unit_copy(s, False).wait_send()

        return carry

    lax.fori_loop(0, n - 1, drain, 0)

    def drain_spill(j, carry):
        for side in range(2):

            @pl.when(sends_spill[side])
            def _(side=side):
                spill_copy(side, j).wait_send()

        return carry

    lax.fori_loop(0, n, drain_spill, 0)


def local(sizes, images, mask_bits, inv_var, routes, block_slot, kernel_index, coefficients):
    n, strips, bands = sizes["exp"], sizes["tile"], sizes["band"]
    held = images.shape[2]
    tile_rows = BLOCK_ROWS * BLOCK
    tile_cols = BLOCK_COLS * BLOCK
    half = tile_cols // 2
    across = tap_pair(tap_matrix(2 * half, half, BLOCK))
    down = tap_pair(tap_matrix(tile_rows + 2 * SPILL, tile_rows, SPILL))
    smem = pl.BlockSpec(memory_space=pltpu.SMEM)
    vmem = pl.BlockSpec(memory_space=pltpu.VMEM)
    depth, basis = pl.pallas_call(
        functools.partial(place_kernel, held),
        grid=(n,),
        out_shape=(
            jax.ShapeDtypeStruct((n, tile_rows, tile_cols), jnp.bfloat16),
            jax.ShapeDtypeStruct((n, 2, 3, tile_rows, tile_cols), jnp.bfloat16),
        ),
        in_specs=[smem] * 5 + [vmem] * 2,
        out_specs=(
            pl.BlockSpec((1, tile_rows, tile_cols), lambda d: (d, 0, 0)),
            pl.BlockSpec((1, 2, 3, tile_rows, tile_cols), lambda d: (d, 0, 0, 0, 0)),
        ),
        scratch_shapes=[pltpu.VMEM((4, tile_rows, tile_cols), jnp.float32)],
        name="place",
    )(
        routes[0, 0, :, 0], block_slot[0, 0], kernel_index[0, 0], inv_var[0, 0],
        coefficients.T, images[0, 0], mask_bits[0, 0],
    )
    whole = jax.ShapeDtypeStruct((tile_rows, tile_cols), jnp.float32)
    others = jax.ShapeDtypeStruct((bands - 1, tile_rows, tile_cols), jnp.float32)
    numerator, denominator, det_mine, det_theirs = pl.pallas_call(
        functools.partial(reduce_kernel, n, strips, bands),
        out_shape=(whole, whole, whole, others),
        in_specs=[vmem, pl.BlockSpec(memory_space=pl.ANY), vmem, vmem],
        out_specs=(vmem,) * 4,
        scratch_shapes=[
            pltpu.VMEM((n + 1, tile_rows, tile_cols), jnp.bfloat16),
            pltpu.VMEM((n, tile_rows, tile_cols), jnp.bfloat16),
            pltpu.VMEM((n, tile_rows, tile_cols), jnp.bfloat16),
            pltpu.VMEM((2, 2, 3, tile_rows, tile_cols + 2 * BLOCK), jnp.bfloat16),
            pltpu.VMEM((2, tile_rows, tile_cols), jnp.float32),
            pltpu.VMEM((2, n, SPILL, tile_cols), jnp.bfloat16),
            pltpu.VMEM((2, n, SPILL, tile_cols), jnp.bfloat16),
            pltpu.SemaphoreType.DMA((n,)),
            pltpu.SemaphoreType.DMA((n + 1,)),
            pltpu.SemaphoreType.DMA((n,)),
            pltpu.SemaphoreType.DMA((n,)),
            pltpu.SemaphoreType.DMA((2, n)),
            pltpu.SemaphoreType.DMA((2, n)),
            pltpu.SemaphoreType.DMA((bands - 1,)),
            pltpu.SemaphoreType.DMA((bands - 1,)),
            pltpu.SemaphoreType.DMA((2, 3)),
        ],
        compiler_params=pltpu.CompilerParams(collective_id=0, has_side_effects=True),
        name="correlate_and_reduce",
    )(depth, basis, across, down)
    return (numerator / denominator)[None], det_mine + jnp.sum(det_theirs, axis=0)


def solution(mesh):
    return jax.shard_map(
        functools.partial(local, dict(mesh.shape)),
        mesh=mesh,
        in_specs=(
            P(("patch", "band"), "tile", "exp", None, None),
            P(("patch", "band"), "tile", "exp", None, None),
            P(("patch", "band"), "tile", "exp"),
            P(("patch", "band"), "tile", "exp", None),
            P(("patch", "band"), "tile", "exp"),
            P(("patch", "band"), "tile", "exp"),
            P(),
        ),
        out_specs=(P(("patch", "band"), "tile", "exp"), P(("patch", "tile"), "exp")),
        check_vma=False,
    )
```

time: 80 us -> 67.9 us (0.85)
  the two profiles are of different devices: /device:TPU:0 before, /device:TPU:25 now
where the time goes in v2:
time: 67.9 us; the launch traced here: 67.7 us
  Pallas kernels  62.9 us (93%)
  other arithmetic  4.16 us (6%)
    pallas_call x1, Pallas kernels, local(): pl.pallas_call(functools.partial(reduce_kernel, n, strips, bands), out_sh...  56.6 us
    pallas_call x1, Pallas kernels, local(): pl.pallas_call(functools.partial(place_kernel, held), grid=(n,), out_shap...  6.3 us
    broadcast_in_dim x1, other arithmetic, local(): (numerator / denominator)[None]  2.08 us
    add x1, other arithmetic, local(): det_mine + jnp.sum(det_theirs, axis=0)  2.07 us

profile of v2, /device:TPU:25, one launch (start us, length us, event | category | flops | bytes accessed | tf_op | source)
XLA Modules:
  0.0 67.7 jit_solution(2373952539294994610)
XLA Ops:
  0.6 6.3 %place.1 = (bf16[4,256,512]{2,1,0:T(8,128)(2,1)}, bf16[4,2,3,256,512]{4,3,2,1,0:T(8,128)(2,1)}) custom-call(s32[16]{0:T(128)} %bitcast.14, s32[16]{0:T(128)} %bitcast.15, s32[16]{0:T(128)} %bitcast.16, f32[16]{0:T(128)} %bitcast.17, f32[3,64]{1,0:T(4,128)} %bitcast.13, bf16[16,128,128]{2,1,0:T(8,128)(2,1)} %bitcast.12, s32[16,128,128]{2,1,0:T(8,128)} %bitcast.11), custom_call_target="tpu_custom_call" | custom-call | tf_op jit(solution)/shard_map/place/pallas_call | solution.py:428
  6.9 56.6 %correlate_and_reduce.1 = (f32[256,512]{1,0:T(8,128)}, f32[256,512]{1,0:T(8,128)}, f32[256,512]{1,0:T(8,128)}, f32[1,256,512]{2,1,0:T(8,128)}) custom-call(bf16[4,256,512]{2,1,0:T(8,128)(2,1)} %get-tuple-element.8.depth, bf16[4,2,3,256,512]{4,3,2,1,0:T(8,128)(2,1)} %get-tuple-element.9.basis, bf16[2,3,512,256]{3,2,1,0:T(8,128)(2,1)} %constant.2.clone.across, ...), custom_call_target="tpu_custom_call" | custom-call | tf_op jit(solution)/shard_map/correlate_and_reduce/pallas_call | solution.py:448
  63.5 2.1 %divide_bitcast_fusion = f32[1,256,512]{2,1,0:T(8,128)} fusion(f32[256,512]{1,0:T(8,128)} %get-tuple-element.10, f32[256,512]{1,0:T(8,128)} %get-tuple-element.11), kind=kLoop, calls=%fused_computation.1 | loop fusion | flops 131072 | bytes 1572864 | tf_op jit(solution)/shard_map/broadcast_in_dim | solution.py:474
  65.6 2.1 %bitcast_add_fusion = f32[256,512]{1,0:T(8,128)} fusion(f32[256,512]{1,0:T(8,128)} %get-tuple-element.12, f32[1,256,512]{2,1,0:T(8,128)} %get-tuple-element.13), kind=kLoop, calls=%fused_computation | loop fusion | flops 131072 | bytes 1572864 | tf_op jit(solution)/shard_map/add | solution.py:474

commit v3 on v2

--- a/solution.py
+++ b/solution.py
@@ -12,7 +12,7 @@
 TAPS = 41
 BLOCK_ROWS = 2
 BLOCK_COLS = 4
-SPILL = 32
+SPILL = 24
 
 kernel_sigmas = (1.0, 2.5, 6.0)
 MESH = pl.DeviceIdType.MESH
@@ -47,10 +47,12 @@
     return high, (value - high.astype(jnp.float32)).astype(jnp.bfloat16)
 
 
-def dot3(left, right):
-    (left_high, left_low), (right_high, right_low) = left, right
-    dot = functools.partial(jnp.dot, preferred_element_type=jnp.float32)
-    return dot(left_high, right_high) + (dot(left_high, right_low) + dot(left_low, right_high))
+def products(pairs):
+    total = None
+    for left, right in pairs:
+        term = jnp.dot(left, right, preferred_element_type=jnp.float32)
+        total = term if total is None else total + term
+    return total
 
 
 def place_kernel(
@@ -82,8 +84,9 @@
 
     lax.fori_loop(0, held, one, 0)
     depth[0] = acc[3].astype(jnp.bfloat16)
-    for k in range(3):
-        basis[0, 0, k], basis[0, 1, k] = split(acc[k])
+    basis[0, 0], basis[0, 1] = split(acc[0])
+    basis[0, 2] = acc[1].astype(jnp.bfloat16)
+    basis[0, 3] = acc[2].astype(jnp.bfloat16)
 
 
 def reduce_kernel(
@@ -131,16 +134,16 @@
         whole = pl.ds(BLOCK, tile_cols)
         return (
             pltpu.make_async_copy(
-                basis.at[d], framed.at[slot, :, :, :, whole], frame_sem.at[slot, 0]
+                basis.at[d], framed.at[slot, :, :, whole], frame_sem.at[slot, 0]
             ),
             pltpu.make_async_copy(
-                basis.at[before, :, :, :, pl.ds(tile_cols - BLOCK, BLOCK)],
-                framed.at[slot, :, :, :, pl.ds(0, BLOCK)],
+                basis.at[before, :, :, pl.ds(tile_cols - BLOCK, BLOCK)],
+                framed.at[slot, :, :, pl.ds(0, BLOCK)],
                 frame_sem.at[slot, 1],
             ),
             pltpu.make_async_copy(
-                basis.at[after, :, :, :, pl.ds(0, BLOCK)],
-                framed.at[slot, :, :, :, pl.ds(BLOCK + tile_cols, BLOCK)],
+                basis.at[after, :, :, pl.ds(0, BLOCK)],
+                framed.at[slot, :, :, pl.ds(BLOCK + tile_cols, BLOCK)],
                 frame_sem.at[slot, 2],
             ),
         )
@@ -171,26 +174,33 @@
 
         @pl.when(d == 0)
         def _():
-            framed[slot, :, :, :, 0:BLOCK] = jnp.zeros(
-                framed.shape[1:4] + (BLOCK,), framed.dtype
+            framed[slot, :, :, 0:BLOCK] = jnp.zeros(
+                framed.shape[1:3] + (BLOCK,), framed.dtype
             )
 
         @pl.when(d == n - 1)
         def _():
-            framed[slot, :, :, :, BLOCK + tile_cols :] = jnp.zeros(
-                framed.shape[1:4] + (BLOCK,), framed.dtype
+            framed[slot, :, :, BLOCK + tile_cols :] = jnp.zeros(
+                framed.shape[1:3] + (BLOCK,), framed.dtype
             )
 
+        first = (framed[slot, 0], framed[slot, 1])
+        tall_high, tall_low = split(
+            products(((down[0, 0], first[0]), (down[0, 0], first[1]), (down[1, 0], first[0])))
+        )
+        second = framed[slot, 2]
+        tall_second = products(((down[0, 1], second), (down[1, 1], second))).astype(jnp.bfloat16)
+        tall_third = products(((down[0, 2], framed[slot, 3]),)).astype(jnp.bfloat16)
         for h in range(2):
-            total = None
-            for k in range(3):
-                cols = slice(h * half, h * half + half + 2 * BLOCK)
-                tall = dot3(
-                    (down[0, k], down[1, k]),
-                    (framed[slot, 0, k, :, cols], framed[slot, 1, k, :, cols]),
-                )
-                term = dot3(split(tall), (across[0, k], across[1, k]))
-                total = term if total is None else total + term
+            cols = slice(h * half, h * half + half + 2 * BLOCK)
+            total = products((
+                (tall_high[:, cols], across[0, 0]),
+                (tall_high[:, cols], across[1, 0]),
+                (tall_low[:, cols], across[0, 0]),
+                (tall_second[:, cols], across[0, 1]),
+                (tall_second[:, cols], across[1, 1]),
+                (tall_third[:, cols], across[0, 2]),
+            ))
             out = slice(h * half, (h + 1) * half)
             result[slot, :, out] = total[SPILL : SPILL + rows_all]
             spilling[0, j, :, out] = total[SPILL + rows_all :].astype(jnp.bfloat16)
@@ -249,15 +259,6 @@
             device_id_type=MESH,
         )
 
-    def edges(j, r):
-        value = None
-        if r < SPILL:
-            value = spilled[0, j, r : r + chunk].astype(jnp.float32)
-        if r >= rows_all - SPILL:
-            low = r - (rows_all - SPILL)
-            value = spilled[1, j, low : low + chunk].astype(jnp.float32)
-        return value
-
     def complete(j, slot):
         for side in range(2):
 
@@ -265,16 +266,14 @@
             def _(side=side):
                 spill_copy(side, j).wait_recv()
 
-        for r in range(0, rows_all, chunk):
-            rows = slice(r, r + chunk)
-            edge = edges(j, r)
-            value = result[slot, rows]
-            if edge is not None:
-                value += edge
-            if isinstance(j, int):
-                numerator[rows] = value
-            else:
-                outgoing[j, rows] = value.astype(jnp.bfloat16)
+        low = rows_all - SPILL
+        result[slot, 0:SPILL] += spilled[0, j].astype(jnp.float32)
+        result[slot, low:] += spilled[1, j].astype(jnp.float32)
+        if isinstance(j, int):
+            numerator[...] = result[slot]
+        else:
+            for r in range(0, rows_all, chunk):
+                outgoing[j, r : r + chunk] = result[slot, r : r + chunk].astype(jnp.bfloat16)
 
     def step_right(s, carry):
         @pl.when(n - 1 - s > me)
@@ -300,6 +299,9 @@
     @pl.when(me == n - 1)
     def _():
         lax.fori_loop(0, n - 1, step_left, 0)
+
+    right_first = 2 * me < n - 1
+    left_first = jnp.logical_not(right_first)
 
     def turn(i, carry):
         j = n - 1 - i
@@ -317,23 +319,33 @@
             complete(j + 1, 1 - slot)
             match_copy(j + 1).start()
 
+        @pl.when((i > 1) & right_first & (me > 0))
+        def _():
+            step_right(i - 2, 0)
+
+        @pl.when((i > 1) & left_first & (me < n - 1))
+        def _():
+            step_left(i - 2, 0)
+
         return carry
 
     lax.fori_loop(0, n, turn, 0)
     complete(0, (n - 1) % 2)
 
-    right_first = 2 * me < n - 1
-
-    @pl.when(right_first & (me > 0))
-    def _():
-        lax.fori_loop(0, n - 1, step_right, 0)
-
-    @pl.when(me < n - 1)
-    def _():
+    @pl.when(right_first)
+    def _():
+        @pl.when(me > 0)
+        def _():
+            lax.fori_loop(max(n - 2, 0), n - 1, step_right, 0)
+
         lax.fori_loop(0, n - 1, step_left, 0)
 
-    @pl.when(jnp.logical_not(right_first) & (me > 0))
-    def _():
+    @pl.when(left_first)
+    def _():
+        @pl.when(me < n - 1)
+        def _():
+            lax.fori_loop(max(n - 2, 0), n - 1, step_left, 0)
+
         lax.fori_loop(0, n - 1, step_right, 0)
 
     @pl.when(me > 0)
@@ -413,6 +425,14 @@
         return carry
 
     lax.fori_loop(0, n, drain_spill, 0)
+
+
+def finish_kernel(numerator, denominator, det_mine, det_theirs, coadd, detection):
+    coadd[...] = numerator[...] / denominator[...]
+    value = det_mine[...]
+    for j in range(det_theirs.shape[0]):
+        value += det_theirs[j]
+    detection[...] = value
 
 
 def local(sizes, images, mask_bits, inv_var, routes, block_slot, kernel_index, coefficients):
@@ -430,12 +450,12 @@
         grid=(n,),
         out_shape=(
             jax.ShapeDtypeStruct((n, tile_rows, tile_cols), jnp.bfloat16),
-            jax.ShapeDtypeStruct((n, 2, 3, tile_rows, tile_cols), jnp.bfloat16),
+            jax.ShapeDtypeStruct((n, 4, tile_rows, tile_cols), jnp.bfloat16),
         ),
         in_specs=[smem] * 5 + [vmem] * 2,
         out_specs=(
             pl.BlockSpec((1, tile_rows, tile_cols), lambda d: (d, 0, 0)),
-            pl.BlockSpec((1, 2, 3, tile_rows, tile_cols), lambda d: (d, 0, 0, 0, 0)),
+            pl.BlockSpec((1, 4, tile_rows, tile_cols), lambda d: (d, 0, 0, 0)),
         ),
         scratch_shapes=[pltpu.VMEM((4, tile_rows, tile_cols), jnp.float32)],
         name="place",
@@ -454,7 +474,7 @@
             pltpu.VMEM((n + 1, tile_rows, tile_cols), jnp.bfloat16),
             pltpu.VMEM((n, tile_rows, tile_cols), jnp.bfloat16),
             pltpu.VMEM((n, tile_rows, tile_cols), jnp.bfloat16),
-            pltpu.VMEM((2, 2, 3, tile_rows, tile_cols + 2 * BLOCK), jnp.bfloat16),
+            pltpu.VMEM((2, 4, tile_rows, tile_cols + 2 * BLOCK), jnp.bfloat16),
             pltpu.VMEM((2, tile_rows, tile_cols), jnp.float32),
             pltpu.VMEM((2, n, SPILL, tile_cols), jnp.bfloat16),
             pltpu.VMEM((2, n, SPILL, tile_cols), jnp.bfloat16),
@@ -471,7 +491,17 @@
         compiler_params=pltpu.CompilerParams(collective_id=0, has_side_effects=True),
         name="correlate_and_reduce",
     )(depth, basis, across, down)
-    return (numerator / denominator)[None], det_mine + jnp.sum(det_theirs, axis=0)
+    part = pl.BlockSpec((tile_rows // 2, tile_cols), lambda i: (i, 0))
+    coadd, detection = pl.pallas_call(
+        finish_kernel,
+        grid=(2,),
+        out_shape=(whole, whole),
+        in_specs=[part] * 3
+        + [pl.BlockSpec((bands - 1, tile_rows // 2, tile_cols), lambda i: (0, i, 0))],
+        out_specs=(part, part),
+        name="finish",
+    )(numerator, denominator, det_mine, det_theirs)
+    return coadd[None], detection
 
 
 def solution(mesh):

time: 67.9 us -> 61.2 us (0.901)
  the two profiles are of different devices: /device:TPU:25 before, /device:TPU:0 now
where the time goes in v3:
time: 61.2 us; the launch traced here: 61 us
  Pallas kernels  60.4 us (99%)
  between operations  0.64 us (1%)
    pallas_call x1, Pallas kernels, local(): pl.pallas_call(functools.partial(reduce_kernel, n, strips, bands), out_sh...  52.3 us
    pallas_call x1, Pallas kernels, local(): pl.pallas_call(functools.partial(place_kernel, held), grid=(n,), out_shap...  5.68 us
    pallas_call x1, Pallas kernels, local(): pl.pallas_call(finish_kernel, grid=(2,), out_shape=(whole, whole), in_spe...  2.37 us

profile of v3, /device:TPU:0, one launch (start us, length us, event | category | flops | bytes accessed | tf_op | source)
XLA Modules:
  0.0 61.0 jit_solution(9047846142015892380)
XLA Ops:
  0.6 5.7 %place.1 = (bf16[4,256,512]{2,1,0:T(8,128)(2,1)}, bf16[4,4,256,512]{3,2,1,0:T(8,128)(2,1)}) custom-call(s32[16]{0:T(128)} %bitcast.11, s32[16]{0:T(128)} %bitcast.12, s32[16]{0:T(128)} %bitcast.13, f32[16]{0:T(128)} %bitcast.14, f32[3,64]{1,0:T(4,128)} %bitcast.10, bf16[16,128,128]{2,1,0:T(8,128)(2,1)} %bitcast.9, s32[16,128,128]{2,1,0:T(8,128)} %bitcast.8), custom_call_target="tpu_custom_call" | custom-call | tf_op jit(solution)/shard_map/place/pallas_call | solution.py:448
  6.3 52.3 %correlate_and_reduce.1 = (f32[256,512]{1,0:T(8,128)}, f32[256,512]{1,0:T(8,128)}, f32[256,512]{1,0:T(8,128)}, f32[1,256,512]{2,1,0:T(8,128)}) custom-call(bf16[4,256,512]{2,1,0:T(8,128)(2,1)} %get-tuple-element.10.depth, bf16[4,4,256,512]{3,2,1,0:T(8,128)(2,1)} %get-tuple-element.11.basis, bf16[2,3,512,256]{3,2,1,0:T(8,128)(2,1)} %constant.4.clone.across, ...), custom_call_target="tpu_custom_call" | custom-call | tf_op jit(solution)/shard_map/correlate_and_reduce/pallas_call | solution.py:468
  58.7 2.4 %finish.1 = (f32[256,512]{1,0:T(8,128)}, f32[256,512]{1,0:T(8,128)}) custom-call(f32[256,512]{1,0:T(8,128)} %get-tuple-element.12.numerator, f32[256,512]{1,0:T(8,128)} %get-tuple-element.13.denominator, f32[256,512]{1,0:T(8,128)} %get-tuple-element.14.det_mine, f32[1,256,512]{2,1,0:T(8,128)} %get-tuple-element.15.det_theirs), custom_call_target="tpu_custom_call" | custom-call | tf_op jit(solution)/shard_map/finish/pallas_call | solution.py:495

commit v4 on v3

--- a/solution.py
+++ b/solution.py
@@ -289,35 +289,43 @@
 
         return carry
 
-    for copy in frame_copies(n - 1, 0):
-        copy.start()
-
-    @pl.when(me == 0)
-    def _():
-        lax.fori_loop(0, n - 1, step_right, 0)
-
-    @pl.when(me == n - 1)
-    def _():
-        lax.fori_loop(0, n - 1, step_left, 0)
-
     right_first = 2 * me < n - 1
     left_first = jnp.logical_not(right_first)
 
+    def pick(i):
+        down_from = n - 1 - i
+        right = jnp.where(down_from > me, down_from, down_from - 1)
+        left = jnp.where(i < me, i, i + 1)
+        d = jnp.where(right_first, right, left)
+        return jnp.where(i == n - 1, 0, lax.rem(d - me + n, n))
+
+    for copy in frame_copies(pick(0), 0):
+        copy.start()
+
+    @pl.when(me == 0)
+    def _():
+        lax.fori_loop(0, n - 1, step_right, 0)
+
+    @pl.when(me == n - 1)
+    def _():
+        lax.fori_loop(0, n - 1, step_left, 0)
+
     def turn(i, carry):
-        j = n - 1 - i
+        j = pick(i)
         slot = lax.rem(i, 2)
 
         @pl.when(i < n - 1)
         def _():
-            for copy in frame_copies(j - 1, 1 - slot):
+            for copy in frame_copies(pick(i + 1), 1 - slot):
                 copy.start()
 
         correlate(j, slot)
 
         @pl.when(i > 0)
         def _():
-            complete(j + 1, 1 - slot)
-            match_copy(j + 1).start()
+            earlier = pick(i - 1)
+            complete(earlier, 1 - slot)
+            match_copy(earlier).start()
 
         @pl.when((i > 1) & right_first & (me > 0))
         def _():
@@ -373,31 +381,33 @@
         return carry
 
     lax.fori_loop(0, n - 1, gather, 0)
-    for r in range(0, rows_all, chunk):
-        rows = slice(r, r + chunk)
-        below = 1.0 + (
-            depth[me, rows].astype(jnp.float32)
-            + moving[me, rows].astype(jnp.float32)
-            + moving[n, rows].astype(jnp.float32)
-        )
-        denominator[rows] = below
-        value = numerator[rows] / below
-        det_mine[rows] = value * value * below
-
-    def det_copy(j):
+    def det_copy(j, h):
+        rows = pl.ds(h * rows_all // 2, rows_all // 2)
         return pltpu.make_async_remote_copy(
-            src_ref=det_mine,
-            dst_ref=det_theirs.at[j - 1],
-            send_sem=det_send.at[j - 1],
-            recv_sem=det_recv.at[j - 1],
+            src_ref=det_mine.at[rows],
+            dst_ref=det_theirs.at[j - 1, rows],
+            send_sem=det_send.at[j - 1, h],
+            recv_sem=det_recv.at[j - 1, h],
             device_id={"band": lax.rem(band + j, bands)},
             device_id_type=MESH,
         )
 
-    for j in range(1, bands):
-        det_copy(j).start()
-    for j in range(1, bands):
-        det_copy(j).wait()
+    for h in range(2):
+        for r in range(h * rows_all // 2, (h + 1) * rows_all // 2, chunk):
+            rows = slice(r, r + chunk)
+            below = 1.0 + (
+                depth[me, rows].astype(jnp.float32)
+                + moving[me, rows].astype(jnp.float32)
+                + moving[n, rows].astype(jnp.float32)
+            )
+            denominator[rows] = below
+            value = numerator[rows] / below
+            det_mine[rows] = value * value * below
+        for j in range(1, bands):
+            det_copy(j, h).start()
+    for h in range(2):
+        for j in range(1, bands):
+            det_copy(j, h).wait()
 
     def drain(s, carry):
         to_right = n - 1 - s
@@ -484,8 +494,8 @@
             pltpu.SemaphoreType.DMA((n,)),
             pltpu.SemaphoreType.DMA((2, n)),
             pltpu.SemaphoreType.DMA((2, n)),
-            pltpu.SemaphoreType.DMA((bands - 1,)),
-            pltpu.SemaphoreType.DMA((bands - 1,)),
+            pltpu.SemaphoreType.DMA((bands - 1, 2)),
+            pltpu.SemaphoreType.DMA((bands - 1, 2)),
             pltpu.SemaphoreType.DMA((2, 3)),
         ],
         compiler_params=pltpu.CompilerParams(collective_id=0, has_side_effects=True),

time: 61.2 us -> 61.2 us (level)
  no operation moved by 1% of the time
where the time goes in v4:
time: 61.2 us; the launch traced here: 61 us
  Pallas kernels  60.4 us (99%)
  between operations  0.64 us (1%)
    pallas_call x1, Pallas kernels, local(): pl.pallas_call(functools.partial(reduce_kernel, n, strips, bands), out_sh...  52.3 us
    pallas_call x1, Pallas kernels, local(): pl.pallas_call(functools.partial(place_kernel, held), grid=(n,), out_shap...  5.73 us
    pallas_call x1, Pallas kernels, local(): pl.pallas_call(finish_kernel, grid=(2,), out_shape=(whole, whole), in_spe...  2.37 us

profile of v4, /device:TPU:0, one launch (start us, length us, event | category | flops | bytes accessed | tf_op | source)
XLA Modules:
  0.0 61.0 jit_solution(10124870098413971272)
XLA Ops:
  0.6 5.7 %place.1 = (bf16[4,256,512]{2,1,0:T(8,128)(2,1)}, bf16[4,4,256,512]{3,2,1,0:T(8,128)(2,1)}) custom-call(s32[16]{0:T(128)} %bitcast.11, s32[16]{0:T(128)} %bitcast.12, s32[16]{0:T(128)} %bitcast.13, f32[16]{0:T(128)} %bitcast.14, f32[3,64]{1,0:T(4,128)} %bitcast.10, bf16[16,128,128]{2,1,0:T(8,128)(2,1)} %bitcast.9, s32[16,128,128]{2,1,0:T(8,128)} %bitcast.8), custom_call_target="tpu_custom_call" | custom-call | tf_op jit(solution)/shard_map/place/pallas_call | solution.py:458
  6.4 52.3 %correlate_and_reduce.1 = (f32[256,512]{1,0:T(8,128)}, f32[256,512]{1,0:T(8,128)}, f32[256,512]{1,0:T(8,128)}, f32[1,256,512]{2,1,0:T(8,128)}) custom-call(bf16[4,256,512]{2,1,0:T(8,128)(2,1)} %get-tuple-element.10.depth, bf16[4,4,256,512]{3,2,1,0:T(8,128)(2,1)} %get-tuple-element.11.basis, bf16[2,3,512,256]{3,2,1,0:T(8,128)(2,1)} %constant.4.clone.across, ...), custom_call_target="tpu_custom_call" | custom-call | tf_op jit(solution)/shard_map/correlate_and_reduce/pallas_call | solution.py:478
  58.7 2.4 %finish.1 = (f32[256,512]{1,0:T(8,128)}, f32[256,512]{1,0:T(8,128)}) custom-call(f32[256,512]{1,0:T(8,128)} %get-tuple-element.12.numerator, f32[256,512]{1,0:T(8,128)} %get-tuple-element.13.denominator, f32[256,512]{1,0:T(8,128)} %get-tuple-element.14.det_mine, f32[1,256,512]{2,1,0:T(8,128)} %get-tuple-element.15.det_theirs), custom_call_target="tpu_custom_call" | custom-call | tf_op jit(solution)/shard_map/finish/pallas_call | solution.py:505

commit v5 on v4

--- a/solution.py
+++ b/solution.py
@@ -327,13 +327,13 @@
             complete(earlier, 1 - slot)
             match_copy(earlier).start()
 
-        @pl.when((i > 1) & right_first & (me > 0))
-        def _():
-            step_right(i - 2, 0)
-
-        @pl.when((i > 1) & left_first & (me < n - 1))
-        def _():
-            step_left(i - 2, 0)
+        @pl.when((i > 0) & right_first & (me > 0))
+        def _():
+            step_right(i - 1, 0)
+
+        @pl.when((i > 0) & left_first & (me < n - 1))
+        def _():
+            step_left(i - 1, 0)
 
         return carry
 
@@ -344,7 +344,7 @@
     def _():
         @pl.when(me > 0)
         def _():
-            lax.fori_loop(max(n - 2, 0), n - 1, step_right, 0)
+            lax.fori_loop(n - 1, n - 1, step_right, 0)
 
         lax.fori_loop(0, n - 1, step_left, 0)
 
@@ -352,7 +352,7 @@
     def _():
         @pl.when(me < n - 1)
         def _():
-            lax.fori_loop(max(n - 2, 0), n - 1, step_left, 0)
+            lax.fori_loop(n - 1, n - 1, step_left, 0)
 
         lax.fori_loop(0, n - 1, step_right, 0)
 
@@ -501,13 +501,13 @@
         compiler_params=pltpu.CompilerParams(collective_id=0, has_side_effects=True),
         name="correlate_and_reduce",
     )(depth, basis, across, down)
-    part = pl.BlockSpec((tile_rows // 2, tile_cols), lambda i: (i, 0))
+    part = pl.BlockSpec((tile_rows // 4, tile_cols), lambda i: (i, 0))
     coadd, detection = pl.pallas_call(
         finish_kernel,
-        grid=(2,),
+        grid=(4,),
         out_shape=(whole, whole),
         in_specs=[part] * 3
-        + [pl.BlockSpec((bands - 1, tile_rows // 2, tile_cols), lambda i: (0, i, 0))],
+        + [pl.BlockSpec((bands - 1, tile_rows // 4, tile_cols), lambda i: (0, i, 0))],
         out_specs=(part, part),
         name="finish",
     )(numerator, denominator, det_mine, det_theirs)

time: 61.2 us -> 59.5 us (0.972)
  the two profiles are of different devices: /device:TPU:0 before, /device:TPU:9 now
where the time goes in v5:
time: 59.5 us; the launch traced here: 59.3 us
  Pallas kernels  58.6 us (98%)
  between operations  0.64 us (1%)
    pallas_call x1, Pallas kernels, local(): pl.pallas_call(functools.partial(reduce_kernel, n, strips, bands), out_sh...  49.3 us
    pallas_call x1, Pallas kernels, local(): pl.pallas_call(functools.partial(place_kernel, held), grid=(n,), out_shap...  5.68 us
    pallas_call x1, Pallas kernels, local(): pl.pallas_call(finish_kernel, grid=(4,), out_shape=(whole, whole), in_spe...  3.62 us

profile of v5, /device:TPU:9, one launch (start us, length us, event | category | flops | bytes accessed | tf_op | source)
XLA Modules:
  0.0 59.3 jit_solution(3649087661309358974)
XLA Ops:
  0.6 5.7 %place.1 = (bf16[4,256,512]{2,1,0:T(8,128)(2,1)}, bf16[4,4,256,512]{3,2,1,0:T(8,128)(2,1)}) custom-call(s32[16]{0:T(128)} %bitcast.11, s32[16]{0:T(128)} %bitcast.12, s32[16]{0:T(128)} %bitcast.13, f32[16]{0:T(128)} %bitcast.14, f32[3,64]{1,0:T(4,128)} %bitcast.10, bf16[16,128,128]{2,1,0:T(8,128)(2,1)} %bitcast.9, s32[16,128,128]{2,1,0:T(8,128)} %bitcast.8), custom_call_target="tpu_custom_call" | custom-call | tf_op jit(solution)/shard_map/place/pallas_call | solution.py:458
  6.3 49.3 %correlate_and_reduce.1 = (f32[256,512]{1,0:T(8,128)}, f32[256,512]{1,0:T(8,128)}, f32[256,512]{1,0:T(8,128)}, f32[1,256,512]{2,1,0:T(8,128)}) custom-call(bf16[4,256,512]{2,1,0:T(8,128)(2,1)} %get-tuple-element.10.depth, bf16[4,4,256,512]{3,2,1,0:T(8,128)(2,1)} %get-tuple-element.11.basis, bf16[2,3,512,256]{3,2,1,0:T(8,128)(2,1)} %constant.4.clone.across, ...), custom_call_target="tpu_custom_call" | custom-call | tf_op jit(solution)/shard_map/correlate_and_reduce/pallas_call | solution.py:478
  55.6 3.6 %finish.1 = (f32[256,512]{1,0:T(8,128)}, f32[256,512]{1,0:T(8,128)}) custom-call(f32[256,512]{1,0:T(8,128)} %get-tuple-element.12.numerator, f32[256,512]{1,0:T(8,128)} %get-tuple-element.13.denominator, f32[256,512]{1,0:T(8,128)} %get-tuple-element.14.det_mine, f32[1,256,512]{2,1,0:T(8,128)} %get-tuple-element.15.det_theirs), custom_call_target="tpu_custom_call" | custom-call | tf_op jit(solution)/shard_map/finish/pallas_call | solution.py:505
